TPU v7x, 32 devices: a whole 2x2x4 slice. The times are simulated.
32 devices in a mesh: patch: 16 (over z, y, x), rep: 2 (over core).
Axes of the slice: x: 2, y: 2, z: 4, core: 2. Of those that a mesh axis runs over, the one named last changes fastest.
Arguments:
- tokens: bfloat16 [8192, 512], P(('patch', 'rep')), may hold values from -6 to 6
- cotangent: bfloat16 [8192, 512], P(('patch', 'rep')), may hold values from -6 to 6
- dest: int32 [8192], P(('patch', 'rep')), may hold values from 0 to 15, as said below
- neighbours: int32 [8192, 16], P(('patch', 'rep')), may hold values from 0 to 8191, as said below
- w_qkv: bfloat16 [512, 1536], replicated, may hold values from -0.25 to 0.25
- w_out: bfloat16 [512, 512], replicated, may hold values from -1 to 1
- w_up: bfloat16 [512, 2048], replicated, may hold values from -0.25 to 0.25
- w_down: bfloat16 [2048, 512], replicated, may hold values from -0.125 to 0.125
- ada_attn: float32 [32, 1024], replicated, may hold values from -0.5 to 0.5
- ada_mlp: float32 [32, 1024], replicated, may hold values from -0.5 to 0.5
- cond: float32 [32], replicated, may hold values from -4 to 4
Outputs:
- output: bfloat16 [8192, 512], P(('patch', 'rep'))
- grad_tokens: bfloat16 [8192, 512], P(('patch', 'rep'))
- grad_qkv: float32 [512, 1536], replicated
- grad_out: float32 [512, 512], replicated
- grad_up: float32 [512, 2048], replicated
- grad_down: float32 [2048, 512], replicated
- grad_ada_attn: float32 [32, 1024], replicated
- grad_ada_mlp: float32 [32, 1024], replicated
- grad_cond: float32 [32], replicated
Inputs may be any that keep to these rules, and one draw needn't show every extreme that they name: `dest`: within each index of rep, every patch receives exactly 256 rows; one device sends at most 17 rows to one patch, and each device sends exactly 17 rows to some patch. neighbours[i, 0] = i; every other neighbour of a node in patch q lies in the rows of the same index of rep in patch q - 1, q or q + 1, counted cyclically over 16 patches; positions may repeat.
All inputs are finite; a program needn't handle non-finite values.
Results may differ from a plain program's by a relative error of at most 0.013.
Values may be sent and summed in bfloat16 or wider, within the bound.
A program may use at most 128 MiB of HBM per device.

v0:
```python
import jax
import jax.numpy as jnp
from jax import lax
from jax.sharding import PartitionSpec as P

H = 4
HD = 128
NEIGH = 16
NORM_EPS = 1e-05


def extended(cells, sides, width):
    for axis, dim in sides:
        count = lax.axis_size(axis)
        head = lax.slice_in_dim(cells, 0, width, axis=dim)
        tail = lax.slice_in_dim(cells, cells.shape[dim] - width, cells.shape[dim], axis=dim)
        cells = jnp.concatenate(
            [
                lax.ppermute(tail, axis, [(i, (i + 1) % count) for i in range(count)]),
                cells,
                lax.ppermute(head, axis, [((i + 1) % count, i) for i in range(count)]),
            ],
            axis=dim,
        )
    return cells


def from_behind(array, axis, by):
    size = lax.axis_size(axis)
    return lax.ppermute(array, axis, [(i, (i + by) % size) for i in range(size)])


def norm_parts(values_in):
    centre = jnp.mean(values_in, axis=-1, keepdims=True)
    centred = values_in - centre
    inverse = lax.rsqrt(jnp.mean(centred * centred, axis=-1, keepdims=True) + NORM_EPS)
    return (centred * inverse, inverse)


def norm_back(grad_normed, plain, inverse, coeffs):
    feature_width = plain.shape[-1]
    scaled = grad_normed * (1.0 + coeffs[:feature_width])
    inner = (
        scaled
        - jnp.mean(scaled, axis=-1, keepdims=True)
        - plain * jnp.mean(scaled * plain, axis=-1, keepdims=True)
    )
    coeff_grad = jnp.concatenate(
        [jnp.sum(grad_normed * plain, axis=0), jnp.sum(grad_normed, axis=0)]
    )
    return (inverse * inner, coeff_grad)


def local(tokens, cotangent, dest, neighbours, w_qkv, w_out, w_up, w_down, ada_attn, ada_mlp, cond):
    highest = lax.Precision.HIGHEST
    row_count = tokens.shape[0]
    feature_width = tokens.shape[1]
    patch_count = lax.axis_size("patch")
    group_count = lax.axis_size("rep")
    capacity = row_count // patch_count + 1
    one_hot = (dest[:, None] == jnp.arange(patch_count, dtype=jnp.int32)[None, :]).astype(jnp.int32)
    earlier = jnp.cumsum(one_hot, axis=0) - one_hot
    slot_index = jnp.sum(earlier * one_hot, axis=1)
    sent_counts = jnp.sum(one_hot, axis=0)
    flat_slot = dest * capacity + slot_index
    outgoing = jnp.zeros((patch_count * capacity, 2 * feature_width), jnp.bfloat16)
    outgoing = outgoing.at[flat_slot].set(jnp.concatenate([tokens, cotangent], axis=1))
    arrived, arrived_counts = (
        lax.all_to_all(
            outgoing.reshape(patch_count, capacity, 2 * feature_width),
            "patch",
            split_axis=0,
            concat_axis=0,
            tiled=True,
        ),
        lax.all_to_all(sent_counts[:, None], "patch", split_axis=0, concat_axis=0, tiled=True),
    )
    counts_in = arrived_counts[:, 0]
    offsets = jnp.cumsum(counts_in) - counts_in
    columns = jnp.arange(capacity, dtype=jnp.int32)
    target = jnp.where(
        columns[None, :] < counts_in[:, None], offsets[:, None] + columns[None, :], row_count
    ).reshape(-1)
    placed = (
        jnp.zeros((row_count + 1, 2 * feature_width), jnp.bfloat16)
        .at[target]
        .set(arrived.reshape(-1, 2 * feature_width))[:row_count]
    )
    node_rows = placed[:, :feature_width].astype(jnp.float32)
    upstream = placed[:, feature_width:]
    coeff_attn = jnp.dot(cond, ada_attn, precision=highest)
    coeff_mlp = jnp.dot(cond, ada_mlp, precision=highest)
    plain_first, inv_first = norm_parts(node_rows)
    normed = (plain_first * (1.0 + coeff_attn[:feature_width]) + coeff_attn[feature_width:]).astype(
        jnp.bfloat16
    )
    projected = jnp.dot(normed, w_qkv, preferred_element_type=jnp.float32)
    queries = projected[:, :feature_width].astype(jnp.bfloat16)
    key_value = projected[:, feature_width:].astype(jnp.bfloat16)
    beside_all = extended(normed, (("patch", 0),), row_count)
    side_rows = jnp.concatenate([beside_all[:row_count], beside_all[2 * row_count :]], axis=0)
    side_kv = jnp.dot(
        side_rows, w_qkv[:, feature_width:], preferred_element_type=jnp.float32
    ).astype(jnp.bfloat16)
    kv_table = jnp.concatenate([side_kv[:row_count], key_value, side_kv[row_count:]], axis=0)
    my_patch = lax.axis_index("patch")
    owners = neighbours // row_count // group_count
    local_row = neighbours % row_count
    rel_patch = (owners - my_patch) % patch_count
    table_index = jnp.where(
        rel_patch == 0,
        row_count + local_row,
        jnp.where(rel_patch == 1, 2 * row_count + local_row, local_row),
    )
    block_rows = min(512, row_count)
    block_count = row_count // block_rows
    score_scale = 1.0 / HD**0.5

    def gather_block(index_block):
        gathered = kv_table[index_block]
        key_block = gathered[..., :feature_width].reshape(block_rows, NEIGH, H, HD)
        value_block = gathered[..., feature_width:].reshape(block_rows, NEIGH, H, HD)
        return (key_block, value_block)

    def forward_block(pieces):
        query_block, index_block = pieces
        key_block, value_block = gather_block(index_block)
        scores = (
            jnp.einsum(
                "bhd,bjhd->bhj",
                query_block.reshape(block_rows, H, HD),
                key_block,
                preferred_element_type=jnp.float32,
            )
            * score_scale
        )
        row_max = jnp.max(scores, axis=-1, keepdims=True)
        row_total = jnp.sum(jnp.exp(scores - row_max), axis=-1, keepdims=True)
        log_total = row_max + jnp.log(row_total)
        weights = jnp.exp(scores - log_total).astype(jnp.bfloat16)
        mixture = jnp.einsum(
            "bhj,bjhd->bhd", weights, value_block, preferred_element_type=jnp.float32
        )
        return (mixture.reshape(block_rows, feature_width).astype(jnp.bfloat16), log_total[..., 0])

    query_blocks = queries.reshape(block_count, block_rows, feature_width)
    index_blocks = table_index.reshape(block_count, block_rows, NEIGH)
    heads_out, log_totals = lax.map(forward_block, (query_blocks, index_blocks))
    heads_out = heads_out.reshape(row_count, feature_width)
    residual = node_rows + jnp.dot(heads_out, w_out, preferred_element_type=jnp.float32)
    plain_second, inv_second = norm_parts(residual)
    normed_mlp = (
        plain_second * (1.0 + coeff_mlp[:feature_width]) + coeff_mlp[feature_width:]
    ).astype(jnp.bfloat16)
    up_proj = jnp.dot(normed_mlp, w_up, preferred_element_type=jnp.float32)
    activation = jax.nn.silu(up_proj).astype(jnp.bfloat16)
    output_rows = residual + jnp.dot(activation, w_down, preferred_element_type=jnp.float32)
    gradient_down = jnp.einsum(
        "ri,rj->ij", activation, upstream, preferred_element_type=jnp.float32
    )
    grad_act = jnp.einsum("rj,ij->ri", upstream, w_down, preferred_element_type=jnp.float32)
    sigmoid_up = jax.nn.sigmoid(up_proj)
    grad_upproj = (grad_act * sigmoid_up * (1.0 + up_proj * (1.0 - sigmoid_up))).astype(
        jnp.bfloat16
    )
    gradient_up = jnp.einsum(
        "ri,rj->ij", normed_mlp, grad_upproj, preferred_element_type=jnp.float32
    )
    grad_normed_mlp = jnp.einsum("rj,ij->ri", grad_upproj, w_up, preferred_element_type=jnp.float32)
    grad_resid_norm, coeff_mlp_grad = norm_back(
        grad_normed_mlp, plain_second, inv_second, coeff_mlp
    )
    grad_residual = upstream.astype(jnp.float32) + grad_resid_norm
    grad_branch = grad_residual.astype(jnp.bfloat16)
    gradient_out = jnp.einsum(
        "ri,rj->ij", heads_out, grad_branch, preferred_element_type=jnp.float32
    )
    grad_heads = jnp.einsum(
        "rj,ij->ri", grad_branch, w_out, preferred_element_type=jnp.float32
    ).astype(jnp.bfloat16)

    def backward_block(table_grad, pieces):
        query_block, index_block, log_block, heads_grad = pieces
        key_block, value_block = gather_block(index_block)
        query_heads = query_block.reshape(block_rows, H, HD)
        scores = (
            jnp.einsum("bhd,bjhd->bhj", query_heads, key_block, preferred_element_type=jnp.float32)
            * score_scale
        )
        weights = jnp.exp(scores - log_block[..., None])
        weights_low = weights.astype(jnp.bfloat16)
        grad_heads_block = heads_grad.reshape(block_rows, H, HD)
        grad_weights = jnp.einsum(
            "bhd,bjhd->bhj", grad_heads_block, value_block, preferred_element_type=jnp.float32
        )
        grad_scores = weights * (
            grad_weights - jnp.sum(weights * grad_weights, axis=-1, keepdims=True)
        )
        scores_low = grad_scores.astype(jnp.bfloat16)
        grad_query = (
            jnp.einsum("bhj,bjhd->bhd", scores_low, key_block, preferred_element_type=jnp.float32)
            * score_scale
        )
        grad_key = (
            jnp.einsum("bhj,bhd->bjhd", scores_low, query_heads, preferred_element_type=jnp.float32)
            * score_scale
        )
        grad_value = jnp.einsum(
            "bhj,bhd->bjhd", weights_low, grad_heads_block, preferred_element_type=jnp.float32
        )
        pair_grad = jnp.concatenate(
            [
                grad_key.reshape(block_rows * NEIGH, feature_width),
                grad_value.reshape(block_rows * NEIGH, feature_width),
            ],
            axis=1,
        )
        table_grad = table_grad.at[index_block.reshape(-1)].add(pair_grad)
        return (table_grad, grad_query.reshape(block_rows, feature_width))

    table_grad, grad_queries = lax.scan(
        backward_block,
        jnp.zeros((3 * row_count, 2 * feature_width), jnp.float32),
        (
            query_blocks,
            index_blocks,
            log_totals,
            grad_heads.reshape(block_count, block_rows, feature_width),
        ),
    )
    returned = table_grad[row_count : 2 * row_count]
    for shift_by, side_piece in ((-1, table_grad[:row_count]), (1, table_grad[2 * row_count :])):
        returned = returned + from_behind(
            side_piece.astype(jnp.bfloat16), "patch", shift_by
        ).astype(side_piece.dtype)
    grad_projected = jnp.concatenate(
        [grad_queries.reshape(row_count, feature_width), returned], axis=1
    ).astype(jnp.bfloat16)
    gradient_proj = jnp.einsum(
        "ri,rj->ij", normed, grad_projected, preferred_element_type=jnp.float32
    )
    grad_normed = jnp.einsum("rj,ij->ri", grad_projected, w_qkv, preferred_element_type=jnp.float32)
    grad_input_norm, coeff_attn_grad = norm_back(grad_normed, plain_first, inv_first, coeff_attn)
    grad_input = (grad_residual + grad_input_norm).astype(jnp.bfloat16)
    gradient_proj, gradient_out, gradient_up, gradient_down, coeff_attn_grad, coeff_mlp_grad = (
        lax.psum(
            (
                gradient_proj,
                gradient_out,
                gradient_up,
                gradient_down,
                coeff_attn_grad,
                coeff_mlp_grad,
            ),
            ("patch", "rep"),
        )
    )
    gradient_ada_attn = jnp.outer(cond, coeff_attn_grad)
    gradient_ada_mlp = jnp.outer(cond, coeff_mlp_grad)
    gradient_cond = jnp.dot(ada_attn, coeff_attn_grad, precision=highest) + jnp.dot(
        ada_mlp, coeff_mlp_grad, precision=highest
    )
    leaving = jnp.concatenate([output_rows.astype(jnp.bfloat16), grad_input], axis=1)
    padded = jnp.concatenate([leaving, jnp.zeros((1, 2 * feature_width), jnp.bfloat16)], axis=0)
    going_back = padded[target].reshape(patch_count, capacity, 2 * feature_width)
    home_rows = lax.all_to_all(
        going_back, "patch", split_axis=0, concat_axis=0, tiled=True
    ).reshape(-1, 2 * feature_width)
    band_rows = home_rows[flat_slot]
    return (
        band_rows[:, :feature_width],
        band_rows[:, feature_width:],
        gradient_proj,
        gradient_out,
        gradient_up,
        gradient_down,
        gradient_ada_attn,
        gradient_ada_mlp,
        gradient_cond,
    )


def solution(mesh):
    return jax.shard_map(
        local,
        mesh=mesh,
        in_specs=(
            P(("patch", "rep"), None),
            P(("patch", "rep"), None),
            P(("patch", "rep")),
            P(("patch", "rep"), None),
            P(),
            P(),
            P(),
            P(),
            P(),
            P(),
            P(),
        ),
        out_specs=(
            P(("patch", "rep"), None),
            P(("patch", "rep"), None),
            P(),
            P(),
            P(),
            P(),
            P(),
            P(),
            P(),
        ),
        check_vma=False,
    )
```

profile of v0, /device:TPU:0, one launch (start us, length us, event | category | flops | bytes accessed | tf_op | source)
XLA Modules:
  0.0 489.2 jit_solution(324026931602704912)
XLA Ops:
  10.4 8.3 %all-to-all-start = ((s32[16,1,1]{2,1,0:T(1,128)}), s32[16,1,1]{2,1,0:T(1,128)S(1)}, u32[]{:S(2)}, u32[]{:S(2)}) async-start(s32[16,1,1]{2,1,0:T(1,128)} %copy.43), calls=%async_computation | async-start | bytes 16384 | tf_op jit(solution)/shard_map/all_to_all | solution.py:76
  26.0 5.3 %all-to-all-start.1 = ((bf16[16,17,1024]{2,1,0:T(8,128)(2,1)}), bf16[16,17,1024]{2,1,0:T(8,128)(2,1)S(1)}, u32[]{:S(2)}, u32[]{:S(2)}) async-start(bf16[16,17,1024]{2,1,0:T(8,128)(2,1)} %reshape.284), calls=%async_computation.1 | async-start | bytes 1572864 | tf_op jit(solution)/shard_map/all_to_all | solution.py:69
  32.7 17.8 %all-to-all-done.1 = bf16[16,17,1024]{2,1,0:T(8,128)(2,1)S(1)} async-done(((bf16[16,17,1024]{2,1,0:T(8,128)(2,1)}), bf16[16,17,1024]{2,1,0:T(8,128)(2,1)S(1)}, u32[]{:S(2)}, u32[]{:S(2)}) %all-to-all-start.1) | async-done | bytes 557088 | tf_op jit(solution)/shard_map/all_to_all | solution.py:69
  55.1 5.5 %collective-permute-start.1 = (bf16[256,512]{1,0:T(8,128)(2,1)S(1)}, bf16[256,512]{1,0:T(8,128)(2,1)}, u32[]{:S(2)}, u32[]{:S(2)}) collective-permute-start(bf16[256,512]{1,0:T(8,128)(2,1)S(1)} %fusion.38), channel_id=1, source_target_pairs={{2,0},{4,2},{6,4},{8,6},{10,8},{12,10},{14,12},{16,14},{18,16},{20... | collective-permute-start | bytes 786440 | tf_op jit(solution)/shard_map/ppermute | solution.py:21
  70.6 22.5 %gather_fusion = bf16[4096,1024]{1,0:T(8,128)(2,1)} fusion(bf16[768,1024]{1,0:T(8,128)(2,1)} %pad_maximum_fusion, s32[4096]{0:T(1024)S(1)} %broadcast_clamp_fusion), kind=kCustom, calls=%fused_computation | custom fusion | bytes 16793600 | tf_op jit(solution)/shard_map/while/body/eval_jaxpr/gather | solution.py:120
  93.1 5.9 %slice_bitcast_fusion = (bf16[256,2,4,8,128]{4,3,2,1,0:T(8,128)(2,1)}, bf16[256,2,4,8,128]{4,3,2,1,0:T(8,128)(2,1)S(1)}) fusion(bf16[256,16,1024]{2,1,0:T(8,128)(2,1)} %bitcast.129), kind=kLoop, calls=%fused_computation.22 | loop fusion | bytes 16777216
  105.5 3.5 fusion.7
  116.6 3.6 fusion.93
  126.9 4.4 fusion.9
  131.2 4.9 %multiply_multiply_fusion = f32[256,4,128,16]{2,1,3,0:T(4,128)S(1)} fusion(f32[256,4,16]{1,2,0:T(8,128)S(1)} %copy-done.2, f32[256,4,128]{2,1,0:T(4,128)S(1)} %copy-done.13), kind=kLoop, calls=%fused_computation.13 | loop fusion | flops 4194304 | bytes 8978432 | tf_op jit(solution)/shard_map/while/body/eval_jaxpr/mul | solution.py:205
  136.2 4.2 copy.98
  140.4 2.4 copy.49
  142.8 6.0 %broadcast_multiply_fusion = f32[256,4,128,16]{2,1,3,0:T(4,128)S(1)} fusion(f32[256,4,16]{1,2,0:T(8,128)} %copy.49, f32[256,4,128]{2,1,0:T(4,128)S(1)} %convert.31), kind=kLoop, calls=%fused_computation.24 | loop fusion | flops 2097152 | bytes 8978432 | tf_op jit(solution)/shard_map/while/body/eval_jaxpr/bhj,bhd->bjhd/dot_general | solution.py:208
  148.8 4.2 copy.97
  153.0 37.3 %scatter_custom_fusion.2 = f32[768,1024]{1,0:T(8,128)} fusion(s32[4096]{0:T(1024)} %bitcast.145, f32[4096,512]{1,0:T(8,128)} %bitcast.128, f32[]{:T(128)} %constant.147.clone.1, f32[4096,512]{1,0:T(8,128)} %bitcast.127, f32[]{:T(128)} %constant.132.clone.1), kind=kCustom, calls=%fused_computation.7 | custom fusion | flops 8388608 | bytes 19923968 | tf_op jit(solution)/shard_map/while/body/eval_jaxpr/scatter-add | solution.py:218
  192.5 3.5 collective-permute-start.2
  196.2 2.8 fusion.63
  199.1 8.3 %collective-permute-done.2 = bf16[256,1024]{1,0:T(8,128)(2,1)S(1)} collective-permute-done((bf16[256,1024]{1,0:T(8,128)(2,1)S(1)}, bf16[256,1024]{1,0:T(8,128)(2,1)S(1)}, u32[]{:S(2)}, u32[]{:S(2)}) %collective-permute-start.2) | collective-permute-done | bytes 524320 | tf_op jit(solution)/shard_map/ppermute | solution.py:30
  207.4 9.9 %collective-permute-done.3 = bf16[256,1024]{1,0:T(8,128)(2,1)S(1)} collective-permute-done((bf16[256,1024]{1,0:T(8,128)(2,1)S(1)}, bf16[256,1024]{1,0:T(8,128)(2,1)S(1)}, u32[]{:S(2)}, u32[]{:S(2)}) %collective-permute-start.3) | collective-permute-done | bytes 524320 | tf_op jit(solution)/shard_map/ppermute | solution.py:30
  221.7 3.1 fusion.20
  229.2 5.3 %all-to-all-start.2 = ((bf16[16,17,1024]{2,1,0:T(8,128)(2,1)}), bf16[16,17,1024]{2,1,0:T(8,128)(2,1)S(1)}, u32[]{:S(2)}, u32[]{:S(2)}) async-start(bf16[16,17,1024]{2,1,0:T(8,128)(2,1)} %reshape.294), calls=%async_computation.2 | async-start | bytes 1572864 | tf_op jit(solution)/shard_map/all_to_all | solution.py:266
  234.6 49.8 %all-reduce.1 = (f32[1024]{0:T(1024)S(1)}, f32[1024]{0:T(1024)S(1)}) all-reduce(f32[1024]{0:T(1024)S(1)} %pad_maximum_fusion.4, f32[1024]{0:T(1024)S(1)} %pad_maximum_fusion.5), channel_id=1, replica_groups=mesh['patch'=16,'rep'=2] {'patch','rep'}, use_global_device_ids=true, to_apply=%region_25.26 | all-reduce | flops 2048 | bytes 16384 | tf_op jit(solution)/shard_map/psum | solution.py:246
  288.4 182.0 %all-reduce.5.cloned.1.call-done = (f32[512,1536]{1,0:T(8,128)}, f32[512,512]{1,0:T(8,128)}, f32[512,2048]{1,0:T(8,128)}, f32[2048,512]{1,0:T(8,128)}) async-done(((f32[512,1536]{1,0:T(8,128)}, f32[512,512]{1,0:T(8,128)}, f32[512,2048]{1,0:T(8,128)}, f32[2048,512]{1,0:T(8,128)}), (f32[512,1536]{1,0:T(8,128)}, f32[512,512]{1,0:T(8,128)}, f32[512,2048]{1,0:T(8,128)}, ...) | async-done | bytes 12582928 | tf_op jit(solution)/shard_map/psum | solution.py:246
  470.4 3.9 copy.104
  (200 shorter events, 69.7 us)
Async XLA Ops:
  7.2 103.3 %copy-start = (bf16[512,2048]{1,0:T(8,128)(2,1)S(1)}, bf16[512,2048]{1,0:T(8,128)(2,1)}, u32[]{:S(2)}) copy-start(bf16[512,2048]{1,0:T(8,128)(2,1)} %param.17) | copy-start | bytes 6291460
  7.2 15.7 %copy-start.21 = (f32[32,1024]{1,0:T(8,128)S(1)}, f32[32,1024]{1,0:T(8,128)}, u32[]{:S(2)}) copy-start(f32[32,1024]{1,0:T(8,128)} %param.19) | copy-start | bytes 393220
  7.2 15.7 %copy-start.40 = (f32[32]{0:T(128)S(1)}, f32[32]{0:T(128)}, u32[]{:S(2)}) copy-start(f32[32]{0:T(128)} %param.21) | copy-start | bytes 388
  7.2 15.9 %copy-start.33 = (s32[256,16]{0,1:T(8,128)S(1)}, s32[256,16]{0,1:T(8,128)}, u32[]{:S(2)}) copy-start(s32[256,16]{0,1:T(8,128)} %param.14) | copy-start | bytes 49156
  7.2 16.1 %copy-start.23 = (f32[32,1024]{1,0:T(8,128)S(1)}, f32[32,1024]{1,0:T(8,128)}, u32[]{:S(2)}) copy-start(f32[32,1024]{1,0:T(8,128)} %param.20) | copy-start | bytes 393220
  10.4 15.5 %all-to-all-start = ((s32[16,1,1]{2,1,0:T(1,128)}), s32[16,1,1]{2,1,0:T(1,128)S(1)}, u32[]{:S(2)}, u32[]{:S(2)}) async-start(s32[16,1,1]{2,1,0:T(1,128)} %copy.43), calls=%async_computation | async-start | bytes 16384 | tf_op jit(solution)/shard_map/all_to_all | solution.py:76
  23.1 31.2 %copy-start.29 = (f32[512]{0:T(512)}, f32[512]{0:T(512)S(1)}, u32[]{:S(2)}) copy-start(f32[512]{0:T(512)S(1)} %get-tuple-element.81) | copy-start | bytes 6148
  26.0 24.5 %all-to-all-start.1 = ((bf16[16,17,1024]{2,1,0:T(8,128)(2,1)}), bf16[16,17,1024]{2,1,0:T(8,128)(2,1)S(1)}, u32[]{:S(2)}, u32[]{:S(2)}) async-start(bf16[16,17,1024]{2,1,0:T(8,128)(2,1)} %reshape.284), calls=%async_computation.1 | async-start | bytes 1572864 | tf_op jit(solution)/shard_map/all_to_all | solution.py:69
  31.3 439.1 %all-reduce.5.cloned.1.call-start = ((), (), s32[]{:S(2)}) async-start(), calls=%async_computation.3 | async-start | bytes 25165824 | tf_op jit(solution)/shard_map/psum | solution.py:246
  32.7 21.6 %copy-start.38 = (s32[272]{0:T(512)}, s32[272]{0:T(512)S(1)}, u32[]{:S(2)}) copy-start(s32[272]{0:T(512)S(1)} %fusion.84) | copy-start | bytes 3268
  54.5 10.9 %collective-permute-start = (bf16[256,512]{1,0:T(8,128)(2,1)S(1)}, bf16[256,512]{1,0:T(8,128)(2,1)}, u32[]{:S(2)}, u32[]{:S(2)}) collective-permute-start(bf16[256,512]{1,0:T(8,128)(2,1)S(1)} %fusion.38), channel_id=1, source_target_pairs={{0,2},{2,4},{4,6},{6,8},{8,10},{10,12},{12,14},{14,16},{16,18},{18... | collective-permute-start | bytes 786440 | tf_op jit(solution)/shard_map/ppermute | solution.py:19
  55.1 12.1 %collective-permute-start.1 = (bf16[256,512]{1,0:T(8,128)(2,1)S(1)}, bf16[256,512]{1,0:T(8,128)(2,1)}, u32[]{:S(2)}, u32[]{:S(2)}) collective-permute-start(bf16[256,512]{1,0:T(8,128)(2,1)S(1)} %fusion.38), channel_id=1, source_target_pairs={{2,0},{4,2},{6,4},{8,6},{10,8},{12,10},{14,12},{16,14},{18,16},{20... | collective-permute-start | bytes 786440 | tf_op jit(solution)/shard_map/ppermute | solution.py:21
  93.1 7.9 %copy-start.19 = (bf16[256,4,128,1]{2,3,1,0:T(2,128)(2,1)S(1)}, bf16[256,4,128,1]{2,3,1,0:T(2,128)(2,1)}, u32[]{:S(2)}) copy-start(bf16[256,4,128,1]{2,3,1,0:T(2,128)(2,1)} %reshape.365) | copy-start | bytes 786436
  116.6 5.0 %copy-start.6 = (bf16[256,2,4,8,128]{4,3,2,1,0:T(8,128)(2,1)S(1)}, bf16[256,2,4,8,128]{4,3,2,1,0:T(8,128)(2,1)}, u32[]{:S(2)}) copy-start(bf16[256,2,4,8,128]{4,3,2,1,0:T(8,128)(2,1)} %get-tuple-element.69) | copy-start | bytes 12582916
  190.2 5.8 %copy-start.18 = (f32[256,4,1,128]{3,2,1,0:T(1,128)S(1)}, f32[256,4,1,128]{3,2,1,0:T(1,128)}, u32[]{:S(2)}) copy-start(f32[256,4,1,128]{3,2,1,0:T(1,128)} %fusion.9) | copy-start | bytes 1572868
  192.5 14.9 %collective-permute-start.2 = (bf16[256,1024]{1,0:T(8,128)(2,1)S(1)}, bf16[256,1024]{1,0:T(8,128)(2,1)S(1)}, u32[]{:S(2)}, u32[]{:S(2)}) collective-permute-start(bf16[256,1024]{1,0:T(8,128)(2,1)S(1)} %get-tuple-element.71), channel_id=1, source_target_pairs={{0,30},{2,0},{4,2},{6,4},{8,6},{10,8},{12,10},{14,12},{16,14},{18,... | collective-permute-start | bytes 1572872 | tf_op jit(solution)/shard_map/ppermute | solution.py:30
  196.0 21.2 %collective-permute-start.3 = (bf16[256,1024]{1,0:T(8,128)(2,1)S(1)}, bf16[256,1024]{1,0:T(8,128)(2,1)S(1)}, u32[]{:S(2)}, u32[]{:S(2)}) collective-permute-start(bf16[256,1024]{1,0:T(8,128)(2,1)S(1)} %get-tuple-element.72), channel_id=1, source_target_pairs={{0,2},{2,4},{4,6},{6,8},{8,10},{10,12},{12,14},{14,16},{16,18},{18... | collective-permute-start | bytes 1572872 | tf_op jit(solution)/shard_map/ppermute | solution.py:30
  228.0 6.5 %copy-start.43 = (s32[256]{0:T(256)S(1)}, s32[256]{0:T(256)}, u32[]{:S(2)}) copy-start(s32[256]{0:T(256)} %copy-done.42) | copy-start | bytes 3076
  228.1 6.5 %copy-start.44 = (f32[512]{0:T(512)S(1)}, f32[512]{0:T(512)}, u32[]{:S(2)}) copy-start(f32[512]{0:T(512)} %get-tuple-element.45) | copy-start | bytes 6148
  228.1 6.5 %copy-start.45 = (f32[512]{0:T(512)S(1)}, f32[512]{0:T(512)}, u32[]{:S(2)}) copy-start(f32[512]{0:T(512)} %get-tuple-element.57) | copy-start | bytes 6148
  228.1 56.4 %copy-start.22 = (f32[32,1024]{1,0:T(8,128)S(1)}, f32[32,1024]{1,0:T(8,128)}, u32[]{:S(2)}) copy-start(f32[32,1024]{1,0:T(8,128)} %param.19) | copy-start | bytes 393220
  228.1 56.5 %copy-start.24 = (f32[32,1024]{1,0:T(8,128)S(1)}, f32[32,1024]{1,0:T(8,128)}, u32[]{:S(2)}) copy-start(f32[32,1024]{1,0:T(8,128)} %param.20) | copy-start | bytes 393220
  228.1 57.3 %copy-start.41 = (f32[32]{0:T(128)S(1)}, f32[32]{0:T(128)}, u32[]{:S(2)}) copy-start(f32[32]{0:T(128)} %param.21) | copy-start | bytes 388
  229.2 57.0 %all-to-all-start.2 = ((bf16[16,17,1024]{2,1,0:T(8,128)(2,1)}), bf16[16,17,1024]{2,1,0:T(8,128)(2,1)S(1)}, u32[]{:S(2)}, u32[]{:S(2)}) async-start(bf16[16,17,1024]{2,1,0:T(8,128)(2,1)} %reshape.294), calls=%async_computation.2 | async-start | bytes 1572864 | tf_op jit(solution)/shard_map/all_to_all | solution.py:266
  (32 other events, 87.3 us)
Sparse Core Ops, SparseCore 0:
  221.2 249.1 all-reduce.4
where the time goes:
time: 494 us; the launch traced here: 489 us
  waiting for transfers between devices  221 us (45%)
  local copies, waits for them, and re-layouts  74.2 us (15%)
  other arithmetic  64.3 us (13%)
  blocking collectives  49.8 us (10%)
  matrix products  35.6 us (7%)
  starting transfers between devices  28.7 us (6%)
  between operations  15.1 us (3%)
    psum x1, waiting for transfers between devices, local(): lax.psum((gradient_proj, gradient_out, gradient_up, gradient_down, coeff_...  182 us
    psum x1, blocking collectives, local(): lax.psum((gradient_proj, gradient_out, gradient_up, gradient_down, coeff_...  49.8 us
    scatter-add x1, other arithmetic, backward_block(): table_grad = table_grad.at[index_block.reshape(-1)].add(pair_grad)  37.3 us
    unnamed x102, local copies, waits for them, and re-layouts  31.4 us
    gather x1, local copies, waits for them, and re-layouts, gather_block(): gathered = kv_table[index_block]  22.5 us
    ppermute x2, waiting for transfers between devices, from_behind(): lax.ppermute(array, axis, [(i, (i + by) % size) for i in range(size)])  18.2 us
    all_to_all x1, waiting for transfers between devices, local(): lax.all_to_all(outgoing.reshape(patch_count, capacity, 2 * feature_width)...  17.8 us
  transfers between devices with their start and end apart: 8, of which 6 were waited for; matrix products, arithmetic and copies ran while one was open for 5% of the time, Pallas kernels for 0%

commit v1 on v0

--- a/solution.py
+++ b/solution.py
@@ -7,6 +7,11 @@
 HD = 128
 NEIGH = 16
 NORM_EPS = 1e-05
+
+
+def one_after_other(value, one, other):
+    half = lax.psum(value, one)
+    return lax.psum(half, other)
 
 
 def extended(cells, sides, width):
@@ -243,7 +248,7 @@
     grad_input_norm, coeff_attn_grad = norm_back(grad_normed, plain_first, inv_first, coeff_attn)
     grad_input = (grad_residual + grad_input_norm).astype(jnp.bfloat16)
     gradient_proj, gradient_out, gradient_up, gradient_down, coeff_attn_grad, coeff_mlp_grad = (
-        lax.psum(
+        one_after_other(
             (
                 gradient_proj,
                 gradient_out,
@@ -252,7 +257,8 @@
                 coeff_attn_grad,
                 coeff_mlp_grad,
             ),
-            ("patch", "rep"),
+            "rep",
+            "patch",
         )
     )
     gradient_ada_attn = jnp.outer(cond, coeff_attn_grad)

time: 494 us -> 676 us (1.37)
  waiting for transfers between devices: 221 us -> 394 us
  blocking collectives: 49.8 us -> 62.9 us
    psum x1 -> x2, waiting for transfers between devices: 182 us -> 353 us  [the longest x1 304 us: one_after_other(): return lax.psum(half, other)]
    psum x1 -> x2, blocking collectives: 49.8 us -> 62.9 us  [the longest x1 60.4 us: one_after_other(): return lax.psum(half, other)]
  transfers between devices with their start and end apart: 8 -> 9, of which waited for: 6 -> 7; matrix products, arithmetic and copies ran while one was open for 5% -> 4% of each run, Pallas kernels for 0% -> 0%
where the time goes in v1:
time: 676 us; the launch traced here: 675 us
  waiting for transfers between devices  394 us (58%)
  local copies, waits for them, and re-layouts  74.1 us (11%)
  other arithmetic  64.3 us (10%)
  blocking collectives  62.9 us (9%)
  matrix products  35.6 us (5%)
  starting transfers between devices  29.3 us (4%)
  between operations  14.9 us (2%)
    psum x1, waiting for transfers between devices, one_after_other(): return lax.psum(half, other)  304 us
    psum x1, blocking collectives, one_after_other(): return lax.psum(half, other)  60.4 us
    psum x1, waiting for transfers between devices, one_after_other(): half = lax.psum(value, one)  49.2 us
    scatter-add x1, other arithmetic, backward_block(): table_grad = table_grad.at[index_block.reshape(-1)].add(pair_grad)  37.3 us
    unnamed x102, local copies, waits for them, and re-layouts  31.5 us
    gather x1, local copies, waits for them, and re-layouts, gather_block(): gathered = kv_table[index_block]  22.5 us
    ppermute x2, waiting for transfers between devices, from_behind(): lax.ppermute(array, axis, [(i, (i + by) % size) for i in range(size)])  18.8 us
    all_to_all x1, waiting for transfers between devices, local(): lax.all_to_all(outgoing.reshape(patch_count, capacity, 2 * feature_width)...  17.8 us
  transfers between devices with their start and end apart: 9, of which 7 were waited for; matrix products, arithmetic and copies ran while one was open for 4% of the time, Pallas kernels for 0%

profile of v1, /device:TPU:0, one launch (start us, length us, event | category | flops | bytes accessed | tf_op | source)
XLA Modules:
  0.0 675.1 jit_solution(11039892625412253030)
XLA Ops:
  10.4 8.3 %all-to-all-start = ((s32[16,1,1]{2,1,0:T(1,128)}), s32[16,1,1]{2,1,0:T(1,128)S(1)}, u32[]{:S(2)}, u32[]{:S(2)}) async-start(s32[16,1,1]{2,1,0:T(1,128)} %copy.43), calls=%async_computation | async-start | bytes 16384 | tf_op jit(solution)/shard_map/all_to_all | solution.py:81
  26.0 5.3 all-to-all-start.1
  32.7 17.8 %all-to-all-done.1 = bf16[16,17,1024]{2,1,0:T(8,128)(2,1)S(1)} async-done(((bf16[16,17,1024]{2,1,0:T(8,128)(2,1)}), bf16[16,17,1024]{2,1,0:T(8,128)(2,1)S(1)}, u32[]{:S(2)}, u32[]{:S(2)}) %all-to-all-start.1) | async-done | bytes 557088 | tf_op jit(solution)/shard_map/all_to_all | solution.py:74
  55.1 5.1 collective-permute-start.1
  70.6 22.5 %gather_fusion = bf16[4096,1024]{1,0:T(8,128)(2,1)} fusion(bf16[768,1024]{1,0:T(8,128)(2,1)} %pad_maximum_fusion, s32[4096]{0:T(1024)S(1)} %broadcast_clamp_fusion), kind=kCustom, calls=%fused_computation | custom fusion | bytes 16793600 | tf_op jit(solution)/shard_map/while/body/eval_jaxpr/gather | solution.py:125
  93.1 5.9 slice_bitcast_fusion
  105.5 3.5 fusion.7
  116.5 3.6 fusion.93
  126.8 4.4 fusion.9
  131.2 4.9 multiply_multiply_fusion
  136.1 4.2 copy.98
  142.7 6.0 broadcast_multiply_fusion
  148.7 4.2 copy.97
  152.9 37.3 %scatter_custom_fusion.2 = f32[768,1024]{1,0:T(8,128)} fusion(s32[4096]{0:T(1024)} %bitcast.145, f32[4096,512]{1,0:T(8,128)} %bitcast.128, f32[]{:T(128)} %constant.147.clone.1, f32[4096,512]{1,0:T(8,128)} %bitcast.127, f32[]{:T(128)} %constant.132.clone.1), kind=kCustom, calls=%fused_computation.7 | custom fusion | flops 8388608 | bytes 19923968 | tf_op jit(solution)/shard_map/while/body/eval_jaxpr/scatter-add | solution.py:223
  192.5 3.1 collective-permute-start.2
  195.8 2.8 fusion.63
  198.6 8.8 %collective-permute-done.2 = bf16[256,1024]{1,0:T(8,128)(2,1)S(1)} collective-permute-done((bf16[256,1024]{1,0:T(8,128)(2,1)S(1)}, bf16[256,1024]{1,0:T(8,128)(2,1)S(1)}, u32[]{:S(2)}, u32[]{:S(2)}) %collective-permute-start.2) | collective-permute-done | bytes 524320 | tf_op jit(solution)/shard_map/ppermute | solution.py:35
  207.4 10.0 %collective-permute-done.3 = bf16[256,1024]{1,0:T(8,128)(2,1)S(1)} collective-permute-done((bf16[256,1024]{1,0:T(8,128)(2,1)S(1)}, bf16[256,1024]{1,0:T(8,128)(2,1)S(1)}, u32[]{:S(2)}, u32[]{:S(2)}) %collective-permute-start.3) | collective-permute-done | bytes 524320 | tf_op jit(solution)/shard_map/ppermute | solution.py:35
  221.2 49.2 %all-reduce.10.cloned.1.call-done = (f32[512,1536]{1,0:T(8,128)}, f32[512,512]{1,0:T(8,128)}, f32[512,2048]{1,0:T(8,128)}, f32[2048,512]{1,0:T(8,128)}) async-done(((f32[512,1536]{1,0:T(8,128)}, f32[512,512]{1,0:T(8,128)}, f32[512,2048]{1,0:T(8,128)}, f32[2048,512]{1,0:T(8,128)}), (f32[512,1536]{1,0:T(8,128)}, f32[512,512]{1,0:T(8,128)}, f32[512,2048]{1,0:T(8,128)}, ...) | async-done | bytes 12582928 | tf_op jit(solution)/shard_map/psum | solution.py:13
  271.1 3.1 fusion.20
  278.6 6.8 %all-to-all-start.2 = ((bf16[16,17,1024]{2,1,0:T(8,128)(2,1)}), bf16[16,17,1024]{2,1,0:T(8,128)(2,1)S(1)}, u32[]{:S(2)}, u32[]{:S(2)}) async-start(bf16[16,17,1024]{2,1,0:T(8,128)(2,1)} %reshape.294), calls=%async_computation.2 | async-start | bytes 1572864 | tf_op jit(solution)/shard_map/all_to_all | solution.py:272
  287.9 60.4 %all-reduce.1 = (f32[1024]{0:T(1024)S(1)}, f32[1024]{0:T(1024)S(1)}) all-reduce(f32[1024]{0:T(1024)S(1)} %get-tuple-element.67, f32[1024]{0:T(1024)S(1)} %get-tuple-element.68), channel_id=1, replica_groups=mesh['patch'=16,'rep'=2] {'patch'}, use_global_device_ids=true, to_apply=%region_30.31 | all-reduce | flops 2048 | bytes 16384 | tf_op jit(solution)/shard_map/psum | solution.py:14
  352.3 304.3 %all-reduce.8.cloned.1.call-done = (f32[512,1536]{1,0:T(8,128)}, f32[512,512]{1,0:T(8,128)}, f32[512,2048]{1,0:T(8,128)}, f32[2048,512]{1,0:T(8,128)}) async-done(((f32[512,1536]{1,0:T(8,128)}, f32[512,512]{1,0:T(8,128)}, f32[512,2048]{1,0:T(8,128)}, f32[2048,512]{1,0:T(8,128)}), (f32[512,1536]{1,0:T(8,128)}, f32[512,512]{1,0:T(8,128)}, f32[512,2048]{1,0:T(8,128)}, ...) | async-done | bytes 12582928 | tf_op jit(solution)/shard_map/psum | solution.py:14
  656.6 3.9 copy.108
  (204 shorter events, 75.0 us)
Async XLA Ops:
  7.2 103.3 %copy-start = (bf16[512,2048]{1,0:T(8,128)(2,1)S(1)}, bf16[512,2048]{1,0:T(8,128)(2,1)}, u32[]{:S(2)}) copy-start(bf16[512,2048]{1,0:T(8,128)(2,1)} %param.17) | copy-start | bytes 6291460
  7.2 15.7 %copy-start.21 = (f32[32,1024]{1,0:T(8,128)S(1)}, f32[32,1024]{1,0:T(8,128)}, u32[]{:S(2)}) copy-start(f32[32,1024]{1,0:T(8,128)} %param.19) | copy-start | bytes 393220
  7.2 15.7 %copy-start.40 = (f32[32]{0:T(128)S(1)}, f32[32]{0:T(128)}, u32[]{:S(2)}) copy-start(f32[32]{0:T(128)} %param.21) | copy-start | bytes 388
  7.2 15.9 %copy-start.33 = (s32[256,16]{0,1:T(8,128)S(1)}, s32[256,16]{0,1:T(8,128)}, u32[]{:S(2)}) copy-start(s32[256,16]{0,1:T(8,128)} %param.14) | copy-start | bytes 49156
  7.2 16.1 %copy-start.23 = (f32[32,1024]{1,0:T(8,128)S(1)}, f32[32,1024]{1,0:T(8,128)}, u32[]{:S(2)}) copy-start(f32[32,1024]{1,0:T(8,128)} %param.20) | copy-start | bytes 393220
  10.4 15.5 %all-to-all-start = ((s32[16,1,1]{2,1,0:T(1,128)}), s32[16,1,1]{2,1,0:T(1,128)S(1)}, u32[]{:S(2)}, u32[]{:S(2)}) async-start(s32[16,1,1]{2,1,0:T(1,128)} %copy.43), calls=%async_computation | async-start | bytes 16384 | tf_op jit(solution)/shard_map/all_to_all | solution.py:81
  23.1 31.2 %copy-start.29 = (f32[512]{0:T(512)}, f32[512]{0:T(512)S(1)}, u32[]{:S(2)}) copy-start(f32[512]{0:T(512)S(1)} %get-tuple-element.87) | copy-start | bytes 6148
  26.0 24.5 %all-to-all-start.1 = ((bf16[16,17,1024]{2,1,0:T(8,128)(2,1)}), bf16[16,17,1024]{2,1,0:T(8,128)(2,1)S(1)}, u32[]{:S(2)}, u32[]{:S(2)}) async-start(bf16[16,17,1024]{2,1,0:T(8,128)(2,1)} %reshape.284), calls=%async_computation.1 | async-start | bytes 1572864 | tf_op jit(solution)/shard_map/all_to_all | solution.py:74
  31.3 239.1 %all-reduce.10.cloned.1.call-start = ((), (), s32[]{:S(2)}) async-start(), calls=%async_computation.4 | async-start | bytes 25165824 | tf_op jit(solution)/shard_map/psum | solution.py:13
  32.7 21.6 %copy-start.38 = (s32[272]{0:T(512)}, s32[272]{0:T(512)S(1)}, u32[]{:S(2)}) copy-start(s32[272]{0:T(512)S(1)} %fusion.84) | copy-start | bytes 3268
  54.5 10.4 %collective-permute-start = (bf16[256,512]{1,0:T(8,128)(2,1)S(1)}, bf16[256,512]{1,0:T(8,128)(2,1)}, u32[]{:S(2)}, u32[]{:S(2)}) collective-permute-start(bf16[256,512]{1,0:T(8,128)(2,1)S(1)} %fusion.38), channel_id=1, source_target_pairs={{0,2},{2,4},{4,6},{6,8},{8,10},{10,12},{12,14},{14,16},{16,18},{18... | collective-permute-start | bytes 786440 | tf_op jit(solution)/shard_map/ppermute | solution.py:24
  55.1 12.1 %collective-permute-start.1 = (bf16[256,512]{1,0:T(8,128)(2,1)S(1)}, bf16[256,512]{1,0:T(8,128)(2,1)}, u32[]{:S(2)}, u32[]{:S(2)}) collective-permute-start(bf16[256,512]{1,0:T(8,128)(2,1)S(1)} %fusion.38), channel_id=1, source_target_pairs={{2,0},{4,2},{6,4},{8,6},{10,8},{12,10},{14,12},{16,14},{18,16},{20... | collective-permute-start | bytes 786440 | tf_op jit(solution)/shard_map/ppermute | solution.py:26
  93.1 7.9 %copy-start.19 = (bf16[256,4,128,1]{2,3,1,0:T(2,128)(2,1)S(1)}, bf16[256,4,128,1]{2,3,1,0:T(2,128)(2,1)}, u32[]{:S(2)}) copy-start(bf16[256,4,128,1]{2,3,1,0:T(2,128)(2,1)} %reshape.365) | copy-start | bytes 786436
  190.2 5.4 copy-start.18
  192.5 14.9 %collective-permute-start.2 = (bf16[256,1024]{1,0:T(8,128)(2,1)S(1)}, bf16[256,1024]{1,0:T(8,128)(2,1)S(1)}, u32[]{:S(2)}, u32[]{:S(2)}) collective-permute-start(bf16[256,1024]{1,0:T(8,128)(2,1)S(1)} %get-tuple-element.77), channel_id=1, source_target_pairs={{0,30},{2,0},{4,2},{6,4},{8,6},{10,8},{12,10},{14,12},{16,14},{18,... | collective-permute-start | bytes 1572872 | tf_op jit(solution)/shard_map/ppermute | solution.py:35
  195.6 21.8 %collective-permute-start.3 = (bf16[256,1024]{1,0:T(8,128)(2,1)S(1)}, bf16[256,1024]{1,0:T(8,128)(2,1)S(1)}, u32[]{:S(2)}, u32[]{:S(2)}) collective-permute-start(bf16[256,1024]{1,0:T(8,128)(2,1)S(1)} %get-tuple-element.78), channel_id=1, source_target_pairs={{0,2},{2,4},{4,6},{6,8},{8,10},{10,12},{12,14},{14,16},{16,18},{18... | collective-permute-start | bytes 1572872 | tf_op jit(solution)/shard_map/ppermute | solution.py:35
  221.2 435.4 %all-reduce.8.cloned.1.call-start = ((), (), s32[]{:S(2)}) async-start(), calls=%async_computation.3 | async-start | bytes 25165824 | tf_op jit(solution)/shard_map/psum | solution.py:14
  277.4 7.9 %copy-start.43 = (s32[256]{0:T(256)S(1)}, s32[256]{0:T(256)}, u32[]{:S(2)}) copy-start(s32[256]{0:T(256)} %copy-done.42) | copy-start | bytes 3076
  277.4 8.0 %copy-start.44 = (f32[512]{0:T(512)S(1)}, f32[512]{0:T(512)}, u32[]{:S(2)}) copy-start(f32[512]{0:T(512)} %get-tuple-element.45) | copy-start | bytes 6148
  277.4 8.0 %copy-start.45 = (f32[512]{0:T(512)S(1)}, f32[512]{0:T(512)}, u32[]{:S(2)}) copy-start(f32[512]{0:T(512)} %get-tuple-element.57) | copy-start | bytes 6148
  277.4 70.9 %copy-start.22 = (f32[32,1024]{1,0:T(8,128)S(1)}, f32[32,1024]{1,0:T(8,128)}, u32[]{:S(2)}) copy-start(f32[32,1024]{1,0:T(8,128)} %param.19) | copy-start | bytes 393220
  277.5 71.1 %copy-start.24 = (f32[32,1024]{1,0:T(8,128)S(1)}, f32[32,1024]{1,0:T(8,128)}, u32[]{:S(2)}) copy-start(f32[32,1024]{1,0:T(8,128)} %param.20) | copy-start | bytes 393220
  277.5 71.9 %copy-start.41 = (f32[32]{0:T(128)S(1)}, f32[32]{0:T(128)}, u32[]{:S(2)}) copy-start(f32[32]{0:T(128)} %param.21) | copy-start | bytes 388
  278.6 71.5 %all-to-all-start.2 = ((bf16[16,17,1024]{2,1,0:T(8,128)(2,1)}), bf16[16,17,1024]{2,1,0:T(8,128)(2,1)S(1)}, u32[]{:S(2)}, u32[]{:S(2)}) async-start(bf16[16,17,1024]{2,1,0:T(8,128)(2,1)} %reshape.294), calls=%async_computation.2 | async-start | bytes 1572864 | tf_op jit(solution)/shard_map/all_to_all | solution.py:272
  (33 other events, 92.4 us)
Sparse Core Ops, SparseCore 0:
  221.3 49.0 all-reduce.9
  276.8 379.7 all-reduce.7
